TPU v7x, 32 devices: a whole 2x2x4 slice. The times are simulated.
32 devices in a mesh: span: 8 (over y, x, core), wall: 4 (over z).
Axes of the slice: x: 2, y: 2, z: 4, core: 2. Of those that a mesh axis runs over, the one named last changes fastest.
Arguments:
- moments: float32 [4, 64, 512, 128], P(None, 'span', 'wall'), may hold values from -32 to 32, as said below
- diffusivity: float32 [64, 512, 128], P('span', 'wall'), may hold values from 0.05 to 20
Outputs:
- transported: float32 [4, 64, 512, 128], P(None, 'span', 'wall')
- updated: float32 [4, 64, 512, 128], P(None, 'span', 'wall')
Inputs may be any that keep to these rules, and one draw needn't show every extreme that they name: `moments`: in every cell m_k = w_1 u_1^k + w_2 u_2^k for k = 0..3, with weights w_1, w_2 between 0.5 and 2 and abscissas u_1, u_2 between -2 and 2 that differ by 0.5 or more.
All inputs are finite; a program needn't handle non-finite values.
Results may differ from a plain program's by a relative error of at most 0.0025.
Values sent between devices are 32-bit elements; how exact they have to be, the bound alone decides.
A program may use at most 64 MiB of HBM per device.

v0:
```python
import jax
import jax.numpy as jnp
from jax import lax
from jax.sharding import PartitionSpec as P

courant = 0.2
diffusion_number = 20000.0


def passed_along(block, axis, distance):
    devices = range(lax.axis_size(axis))
    route = [(i - distance, i) for i in devices if i - distance in devices]
    return lax.ppermute(block, axis, route)


def padded(block, sides, width):
    for axis, dim in sides:
        count = lax.axis_size(axis)
        forward = [(i, i + 1) for i in range(count - 1)]
        forward.append((count - 1, 0))
        backward = [(target, source) for source, target in forward]
        low = lax.ppermute(
            lax.slice_in_dim(block, block.shape[dim] - width, None, axis=dim), axis, forward
        )
        high = lax.ppermute(lax.slice_in_dim(block, 0, width, axis=dim), axis, backward)
        block = jnp.concatenate([low, block, high], axis=dim)
    return block


def quadrature(moments):
    moment_zero = moments[0]
    moment_one = moments[1]
    moment_two = moments[2]
    moment_three = moments[3]
    mean_speed = moment_one / moment_zero
    ratio_two = moment_two / moment_zero
    central_two = ratio_two - mean_speed * mean_speed
    central_three = (
        moment_three / moment_zero
        - 3.0 * mean_speed * ratio_two
        + 2.0 * mean_speed * mean_speed * mean_speed
    )
    skewness = central_three / central_two
    radius = jnp.sqrt(0.25 * skewness * skewness + central_two)
    root_low = 0.5 * skewness - radius
    root_high = 0.5 * skewness + radius
    weight_low = moment_zero * root_high / (2.0 * radius)
    weight_high = -moment_zero * root_low / (2.0 * radius)
    return jnp.stack([weight_low, weight_high, mean_speed + root_low, mean_speed + root_high])


def minmod(first_diff, second_diff):
    return jnp.maximum(jnp.minimum(first_diff, second_diff), 0.0) + jnp.minimum(
        jnp.maximum(first_diff, second_diff), 0.0
    )


def directed(state, outgoing):
    node_terms = []
    for node_index in range(2):
        weight_node = state[node_index]
        abscissa = state[node_index + 2]
        if outgoing:
            carried = jnp.maximum(abscissa, 0.0)
        else:
            carried = jnp.minimum(abscissa, 0.0)
        carried_mass = weight_node * carried
        node_terms.append(
            [
                carried_mass,
                carried_mass * abscissa,
                carried_mass * abscissa * abscissa,
                carried_mass * abscissa * abscissa * abscissa,
            ]
        )
    return jnp.stack(
        [node_terms[0][power_index] + node_terms[1][power_index] for power_index in range(4)]
    )


def advance(moments, extended):
    forward_diff = extended[:, 1:] - extended[:, :-1]
    limited_slope = minmod(forward_diff[:, 1:], forward_diff[:, :-1])
    centre = extended[:, 1:-1]
    upper_state = centre + 0.5 * limited_slope
    lower_state = centre - 0.5 * limited_slope
    face_flux = directed(upper_state[:, :-1], True) + directed(lower_state[:, 1:], False)
    return moments - courant * (face_flux[:, 1:] - face_flux[:, :-1])


def shifted_rows(values, offset, fill_value):
    row_count = values.shape[-2]
    pad_shape = values.shape[:-2] + (abs(offset), values.shape[-1])
    padding = jnp.full(pad_shape, fill_value, values.dtype)
    if offset > 0:
        return jnp.concatenate([padding, values[..., : row_count - offset, :]], axis=-2)
    return jnp.concatenate([values[..., -offset:, :], padding], axis=-2)


def reduce_lines(sub_diag, main_diag, super_diag, rhs_stack):
    row_count = main_diag.shape[-2]
    stride = 1
    while stride < row_count:
        sub_low = shifted_rows(sub_diag, stride, 0.0)
        main_low = shifted_rows(main_diag, stride, 1.0)
        super_low = shifted_rows(super_diag, stride, 0.0)
        rhs_low = shifted_rows(rhs_stack, stride, 0.0)
        sub_high = shifted_rows(sub_diag, -stride, 0.0)
        main_high = shifted_rows(main_diag, -stride, 1.0)
        super_high = shifted_rows(super_diag, -stride, 0.0)
        rhs_high = shifted_rows(rhs_stack, -stride, 0.0)
        left_factor = sub_diag / main_low
        right_factor = super_diag / main_high
        new_sub = -left_factor * sub_low
        new_super = -right_factor * super_high
        main_diag = main_diag - left_factor * super_low - right_factor * sub_high
        rhs_stack = rhs_stack - left_factor * rhs_low - right_factor * rhs_high
        sub_diag = new_sub
        super_diag = new_super
        stride = stride * 2
    return rhs_stack / main_diag


def line_coefficients(diffusion, below):
    lower = jnp.concatenate([below, diffusion[:, :-1, :]], axis=1)
    sub_diag = -diffusion_number * lower
    super_diag = -diffusion_number * diffusion
    main_diag = 1.0 + diffusion_number * lower + diffusion_number * diffusion
    return (sub_diag, main_diag, super_diag)


def solve_segments(transported, diffusivity):
    below = passed_along(diffusivity[:, -1:, :], "wall", 1)
    sub_diag, main_diag, super_diag = line_coefficients(diffusivity, below)
    row_count = diffusivity.shape[1]
    row_index = lax.broadcasted_iota(jnp.int32, diffusivity.shape, 1)
    unit_first = (row_index == 0).astype(jnp.float32)
    unit_last = (row_index == row_count - 1).astype(jnp.float32)
    stacked = jnp.concatenate([transported, unit_first[None], unit_last[None]], axis=0)
    solved = reduce_lines(sub_diag, main_diag, super_diag, stacked)
    partial_sol = solved[:4]
    first_resp = solved[4]
    last_resp = solved[5]
    lead_coef = sub_diag[:, 0, :]
    tail_coef = super_diag[:, -1, :]
    ends_local = jnp.concatenate([partial_sol[:, :, 0, :], partial_sol[:, :, -1, :]], axis=0)[None]
    coupling_local = jnp.stack(
        [
            lead_coef * first_resp[:, 0, :],
            lead_coef * first_resp[:, -1, :],
            tail_coef * last_resp[:, 0, :],
            tail_coef * last_resp[:, -1, :],
        ]
    )[None]
    all_ends, all_coupling = (
        lax.all_gather(ends_local, "wall", axis=0, tiled=True),
        lax.all_gather(coupling_local, "wall", axis=0, tiled=True),
    )
    segment_count = lax.axis_size("wall")
    carry_value = jnp.zeros_like(all_ends[0, :4])
    carry_link = jnp.zeros_like(all_coupling[0, 0])
    stored = []
    for segment in range(segment_count):
        first_end = all_ends[segment, :4]
        last_end = all_ends[segment, 4:]
        lead_first = all_coupling[segment, 0]
        lead_last = all_coupling[segment, 1]
        tail_first = all_coupling[segment, 2]
        tail_last = all_coupling[segment, 3]
        pivot_value = 1.0 - lead_first * carry_link
        start_value = (first_end - lead_first * carry_value) / pivot_value
        start_link = tail_first / pivot_value
        carry_value = last_end - lead_last * carry_value + lead_last * carry_link * start_value
        carry_link = tail_last + lead_last * carry_link * start_link
        stored.append((start_value, start_link, carry_value, carry_link))
    next_start = jnp.zeros_like(carry_value)
    starts_solved = [next_start] * segment_count
    ends_solved = [next_start] * segment_count
    for segment in reversed(range(segment_count)):
        start_value, start_link, end_value, end_link = stored[segment]
        ends_solved[segment] = end_value - end_link * next_start
        starts_solved[segment] = start_value - start_link * next_start
        next_start = starts_solved[segment]
    zero_end = jnp.zeros_like(carry_value)
    prev_stack = jnp.stack([zero_end] + ends_solved[:-1])
    next_stack = jnp.stack(starts_solved[1:] + [zero_end])
    own_segment = lax.axis_index("wall")
    prev_end = lax.dynamic_index_in_dim(prev_stack, own_segment, 0, keepdims=False)
    next_first = lax.dynamic_index_in_dim(next_stack, own_segment, 0, keepdims=False)
    lower_term = (lead_coef[None] * prev_end)[:, :, None, :] * first_resp[None]
    upper_term = (tail_coef[None] * next_first)[:, :, None, :] * last_resp[None]
    return partial_sol - lower_term - upper_term


def body(moments, diffusivity):
    extended = padded(quadrature(moments), (("span", 1),), 2)
    transported = advance(moments, extended)
    updated = solve_segments(transported, diffusivity)
    return (transported, updated)


def solution(mesh):
    in_specs = (P(None, "span", "wall", None), P("span", "wall", None))
    out_specs = (P(None, "span", "wall", None), P(None, "span", "wall", None))
    return jax.shard_map(body, mesh=mesh, in_specs=in_specs, out_specs=out_specs, check_vma=False)
```

profile of v0, /device:TPU:0, one launch (start us, length us, event | category | flops | bytes accessed | tf_op | source)
XLA Modules:
  0.0 80.8 jit_solution(3178878893051822082)
XLA Ops:
  0.6 2.8 %copy.32 = f32[4,8,128,128]{3,1,0,2:T(8,128)S(1)} copy(f32[4,8,128,128]{3,2,1,0:T(8,128)} %param.2) | data formatting | bytes 4194304 | tf_op args[0]
  3.4 0.6 multiply_divide_fusion.1
  4.0 0.6 multiply_divide_fusion
  4.6 1.2 %pad_maximum_fusion.5 = (f32[4,2,128,128]{3,1,0,2:T(2,128)}, f32[4,2,128,128]{3,1,0,2:T(2,128)}) fusion(f32[1,8,128,128]{3,1,0,2:T(8,128)S(1)} %get-tuple-element.87, f32[1,8,128,128]{3,1,0,2:T(8,128)S(1)} %get-tuple-element.88, f32[1,8,128,128]{3,1,0,2:T(8,128)S(1)} %get-tuple-element.86, f32[1,8,128,128]{3,1,0,2:T(8,128)S(1)} %get-tuple-element.57), kind=kLoop, calls=%fused_computation.40 | loop fusion | flops 786432 | bytes 3145728 | tf_op jit(solution)/shard_map/slice | solution.py:23
  5.8 3.4 %collective-permute-start.1 = (f32[4,2,128,128]{3,1,0,2:T(2,128)}, f32[4,2,128,128]{3,1,0,2:T(2,128)}, u32[]{:S(2)}, u32[]{:S(2)}) collective-permute-start(f32[4,2,128,128]{3,1,0,2:T(2,128)} %get-tuple-element.90), channel_id=1, source_target_pairs={{4,0},{8,4},{12,8},{16,12},{20,16},{24,20},{28,24},{0,28},{5,1},{9... | collective-permute-start | bytes 1572872 | tf_op jit(solution)/shard_map/ppermute | solution.py:25
  9.2 3.5 %collective-permute-start.2 = (f32[8,1,128]{2,0,1:T(8,128)S(1)}, f32[8,1,128]{2,0,1:T(8,128)S(1)}, u32[]{:S(2)}, u32[]{:S(2)}) collective-permute-start(f32[8,1,128]{2,0,1:T(8,128)S(1)} %copy.46), channel_id=1, source_target_pairs={{0,1},{1,2},{2,3},{4,5},{5,6},{6,7},{8,9},{9,10},{10,11},{12,13},{... | collective-permute-start | bytes 12296 | tf_op jit(solution)/shard_map/ppermute | solution.py:13
  12.7 0.3 copy.45
  13.0 1.0 %collective-permute-done.2 = f32[8,1,128]{2,0,1:T(8,128)S(1)} collective-permute-done((f32[8,1,128]{2,0,1:T(8,128)S(1)}, f32[8,1,128]{2,0,1:T(8,128)S(1)}, u32[]{:S(2)}, u32[]{:S(2)}) %collective-permute-start.2) | collective-permute-done | bytes 4128 | tf_op jit(solution)/shard_map/ppermute | solution.py:13
  14.0 0.4 broadcast_multiply_fusion
  14.9 0.5 multiply_subtract_fusion.12
  15.8 0.2 multiply_subtract_fusion.11
  16.4 0.3 multiply_subtract_fusion.10
  17.1 0.2 multiply_subtract_fusion.9
  17.7 0.2 multiply_subtract_fusion.8
  18.3 0.2 multiply_subtract_fusion.7
  18.7 1.2 %multiply_subtract_fusion.6 = (f32[8,128,128]{2,0,1:T(8,128)S(1)}, f32[8,128,128]{2,0,1:T(8,128)}, f32[8,128,128]{2,0,1:T(8,128)}) fusion(f32[8,64,128]{2,0,1:T(8,128)S(1)} %slice.522, f32[8,128,128]{2,0,1:T(8,128)S(1)} %get-tuple-element.29, f32[8,64,128]{2,0,1:T(8,128)S(1)} %slice.521, f32[8,128,128]{2,0,1:T(8,128)S(1)} %get-tuple-element.27, ...), kind=kLoop, calls=%fused_computation.46 | loop fusion | flops 786432 | bytes 4194304 | tf_op jit(solution)/shard_map/sub | solution.py:116
  19.8 1.0 %collective-permute-done.1 = f32[4,2,128,128]{3,1,0,2:T(2,128)} collective-permute-done((f32[4,2,128,128]{3,1,0,2:T(2,128)}, f32[4,2,128,128]{3,1,0,2:T(2,128)}, u32[]{:S(2)}, u32[]{:S(2)}) %collective-permute-start.1) | collective-permute-done | bytes 524320 | tf_op jit(solution)/shard_map/ppermute | solution.py:25
  20.9 2.0 %collective-permute-done = f32[4,2,128,128]{3,1,0,2:T(2,128)} collective-permute-done((f32[4,2,128,128]{3,1,0,2:T(2,128)}, f32[4,2,128,128]{3,1,0,2:T(2,128)}, u32[]{:S(2)}, u32[]{:S(2)}) %collective-permute-start) | collective-permute-done | bytes 524320 | tf_op jit(solution)/shard_map/ppermute | solution.py:22
  22.8 2.1 %pad_maximum_fusion = f32[4,12,128,128]{3,1,0,2:T(8,128)S(1)} fusion(f32[4,2,128,128]{3,1,0,2:T(2,128)} %collective-permute-done.1, f32[1,8,128,128]{3,1,0,2:T(8,128)S(1)} %get-tuple-element.87, f32[1,8,128,128]{3,1,0,2:T(8,128)S(1)} %get-tuple-element.88, f32[1,8,128,128]{3,1,0,2:T(8,128)S(1)} %get-tuple-element.86, ...), kind=kLoop, calls=%fused_computation.1 | loop fusion | flops 3932160 | bytes 6291456 | tf_op jit(solution)/shard_map/concatenate | solution.py:26
  24.9 1.2 %slice_subtract_fusion = f32[4,11,128,128]{3,1,0,2:T(8,128)S(1)} fusion(f32[4,12,128,128]{3,1,0,2:T(8,128)S(1)} %pad_maximum_fusion), kind=kLoop, calls=%fused_computation | loop fusion | flops 720896 | bytes 8650752 | tf_op jit(solution)/shard_map/sub | solution.py:82
  26.2 2.3 %slice_subtract_fusion.1 = (f32[4,10,128,128]{3,1,0,2:T(8,128)S(1)}, f32[4,10,128,128]{3,1,0,2:T(8,128)S(1)}) fusion(f32[4,12,128,128]{3,1,0,2:T(8,128)S(1)} %pad_maximum_fusion, f32[4,11,128,128]{3,1,0,2:T(8,128)S(1)} %slice_subtract_fusion), kind=kLoop, calls=%fused_computation.4 | loop fusion | flops 5242880 | bytes 13107200 | tf_op jit(solution)/shard_map/sub | solution.py:86
  28.5 1.4 %fusion.57 = (f32[1,9,128,128]{3,1,0,2:T(8,128)}, f32[1,9,128,128]{3,1,0,2:T(8,128)S(1)}, f32[1,9,128,128]{3,1,0,2:T(8,128)S(1)}) fusion(f32[4,10,128,128]{3,1,0,2:T(8,128)S(1)} %get-tuple-element.60), kind=kLoop, calls=%fused_computation.175 | loop fusion | flops 737280 | bytes 4128768 | tf_op jit(solution)/shard_map/add | solution.py:77
  29.9 1.3 %fusion.58 = (f32[1,9,128,128]{3,1,0,2:T(8,128)}, f32[1,9,128,128]{3,1,0,2:T(8,128)S(1)}, f32[1,9,128,128]{3,1,0,2:T(8,128)S(1)}) fusion(f32[4,10,128,128]{3,1,0,2:T(8,128)S(1)} %get-tuple-element.61), kind=kLoop, calls=%fused_computation.176 | loop fusion | flops 737280 | bytes 4128768 | tf_op jit(solution)/shard_map/add | solution.py:77
  31.2 0.9 %multiply_add_fusion.4 = (f32[1,9,128,128]{3,1,0,2:T(8,128)S(1)}, f32[1,9,128,128]{3,1,0,2:T(8,128)S(1)}, f32[1,9,128,128]{3,1,0,2:T(8,128)S(1)}, f32[1,9,128,12...) fusion(f32[1,9,128,128]{3,1,0,2:T(8,128)S(1)} %get-tuple-element.53, ...), kind=kLoop, calls=%fused_computation.27 | loop fusion | flops 2654208 | bytes 8257536 | tf_op jit(solution)/shard_map/add | solution.py:77
  32.1 2.2 %maximum_add_fusion = f32[4,9,128,128]{3,1,0,2:T(8,128)S(1)} fusion(f32[1,9,128,128]{3,1,0,2:T(8,128)S(1)} %get-tuple-element.149, f32[1,9,128,128]{3,1,0,2:T(8,128)S(1)} %get-tuple-element.148, f32[1,9,128,128]{3,1,0,2:T(8,128)S(1)} %get-tuple-element.150, f32[1,9,128,128]{3,1,0,2:T(8,128)} %get-tuple-element.54, ...), kind=kLoop, calls=%fused_computation.2 | loop fusion | flops 4128768 | bytes 7077888 | tf_op jit(solution)/shard_map/add | solution.py:87
  34.3 1.4 %fusion.2 = f32[4,8,128,128]{3,1,0,2:T(8,128)S(1)} fusion(f32[4,9,128,128]{3,1,0,2:T(8,128)S(1)} %maximum_add_fusion, f32[4,8,128,128]{3,2,1,0:T(8,128)S(1)} %copy-done), kind=kLoop, calls=%fused_computation.18 | loop fusion | flops 1572864 | bytes 8388608 | tf_op jit(solution)/shard_map/sub | solution.py:88
  35.7 2.5 %copy.38 = f32[4,8,128,128]{3,2,1,0:T(8,128)} copy(f32[4,8,128,128]{3,1,0,2:T(8,128)S(1)} %fusion.2) | data formatting | bytes 4194304
  38.5 0.2 iota.9
  38.7 0.2 pad_maximum_fusion.1
  38.9 0.4 fusion.65
  39.3 1.3 %multiply_subtract_fusion.5 = f32[6,8,128,128]{3,1,0,2:T(8,128)S(1)} fusion(f32[6,8,127,128]{3,1,0,2:T(8,128)S(1)} %get-tuple-element.85, f32[6,8,127,128]{3,1,0,2:T(8,128)S(1)} %get-tuple-element.84, f32[8,128,128]{2,0,1:T(8,128)S(1)} %get-tuple-element.50, f32[8,128,128]{2,0,1:T(8,128)S(1)} %get-tuple-element.48, ...), kind=kLoop, calls=%fused_computation.13 | loop fusion | flops 4718592 | bytes 13582336 | tf_op jit(solution)/shard_map/sub | solution.py:117
  40.6 0.5 fusion.64
  41.1 1.1 %multiply_subtract_fusion.4 = f32[6,8,128,128]{3,1,0,2:T(8,128)S(1)} fusion(f32[6,8,126,128]{3,1,0,2:T(8,128)S(1)} %get-tuple-element.83, f32[6,8,128,128]{3,1,0,2:T(8,128)S(1)} %multiply_subtract_fusion.5, f32[6,8,126,128]{3,1,0,2:T(8,128)S(1)} %get-tuple-element.82, f32[8,128,128]{2,0,1:T(8,128)S(1)} %get-tuple-element.46, ...), kind=kLoop, calls=%fused_computation.12 | loop fusion | flops 3145728 | bytes 13533184 | tf_op jit(solution)/shard_map/sub | solution.py:117
  42.3 0.5 fusion.63
  42.8 1.1 %multiply_subtract_fusion.3 = f32[6,8,128,128]{3,1,0,2:T(8,128)S(1)} fusion(f32[6,8,124,128]{3,1,0,2:T(8,128)S(1)} %get-tuple-element.81, f32[6,8,128,128]{3,1,0,2:T(8,128)S(1)} %multiply_subtract_fusion.4, f32[6,8,124,128]{3,1,0,2:T(8,128)S(1)} %get-tuple-element.80, f32[8,128,128]{2,0,1:T(8,128)S(1)} %get-tuple-element.42, ...), kind=kLoop, calls=%fused_computation.11 | loop fusion | flops 3145728 | bytes 13434880 | tf_op jit(solution)/shard_map/sub | solution.py:117
  43.9 0.5 fusion.62
  44.4 1.1 %multiply_subtract_fusion.2 = f32[6,8,128,128]{3,1,0,2:T(8,128)S(1)} fusion(f32[6,8,120,128]{3,1,0,2:T(8,128)S(1)} %get-tuple-element.79, f32[6,8,128,128]{3,1,0,2:T(8,128)S(1)} %multiply_subtract_fusion.3, f32[6,8,120,128]{3,1,0,2:T(8,128)S(1)} %get-tuple-element.78, f32[8,128,128]{2,0,1:T(8,128)S(1)} %get-tuple-element.38, ...), kind=kLoop, calls=%fused_computation.10 | loop fusion | flops 3145728 | bytes 13238272 | tf_op jit(solution)/shard_map/sub | solution.py:117
  45.4 0.4 fusion.61
  45.9 1.0 %multiply_subtract_fusion.1 = f32[6,8,128,128]{3,1,0,2:T(8,128)S(1)} fusion(f32[6,8,112,128]{3,1,0,2:T(8,128)S(1)} %get-tuple-element.77, f32[6,8,128,128]{3,1,0,2:T(8,128)S(1)} %multiply_subtract_fusion.2, f32[6,8,112,128]{3,1,0,2:T(8,128)S(1)} %get-tuple-element.76, f32[8,128,128]{2,0,1:T(8,128)S(1)} %get-tuple-element.34, ...), kind=kLoop, calls=%fused_computation.9 | loop fusion | flops 3145728 | bytes 12845056 | tf_op jit(solution)/shard_map/sub | solution.py:117
  46.9 0.4 fusion.60
  47.3 1.0 %multiply_subtract_fusion = f32[6,8,128,128]{3,1,0,2:T(8,128)S(1)} fusion(f32[6,8,96,128]{3,1,0,2:T(8,128)S(1)} %get-tuple-element.75, f32[6,8,128,128]{3,1,0,2:T(8,128)S(1)} %multiply_subtract_fusion.1, f32[6,8,96,128]{3,1,0,2:T(8,128)S(1)} %get-tuple-element.74, f32[8,128,128]{2,0,1:T(8,128)S(1)} %get-tuple-element.30, f32[8,128,128]{2,0,1:T(8,128)S(1)} %get-tuple-element.28), kind=kLoop, calls=%fused_computation.8 | loop fusion | flops 3145728 | bytes 12058624 | tf_op jit(solution)/shard_map/sub | solution.py:117
  48.3 0.2 fusion.59
  48.5 0.8 %copy-done.2 = f32[8,128,128]{2,0,1:T(8,128)S(1)} copy-done((f32[8,128,128]{2,0,1:T(8,128)S(1)}, f32[8,128,128]{2,0,1:T(8,128)}, u32[]{:S(2)}) %copy-start.2) | copy-done | bytes 524312
  49.4 1.2 %subtract_divide_fusion = f32[6,8,128,128]{3,1,0,2:T(8,128)S(1)} fusion(f32[6,8,64,128]{3,1,0,2:T(8,128)S(1)} %get-tuple-element.73, f32[6,8,128,128]{3,1,0,2:T(8,128)S(1)} %multiply_subtract_fusion, f32[6,8,64,128]{3,1,0,2:T(8,128)S(1)} %get-tuple-element.72, f32[8,128,128]{2,0,1:T(8,128)S(1)} %get-tuple-element.24, f32[8,128,128]{2,0,1:T(8,128)S(1)} %copy-done.3, ...), kind=kLoop, calls=%fused_computation.7 | loop fusion | flops 3932160 | bytes 11010048 | tf_op jit(solution)/shard_map/div | solution.py:121
  50.8 13.5 %all-gather.1 = f32[16,8,128]{2,1,0:T(8,128)S(1)} all-gather(f32[4,8,128]{2,1,0:T(8,128)S(1)} %pad_maximum_fusion.8), channel_id=3, replica_groups=mesh['span'=8,'wall'=4] {'wall'}, dimensions={0}, use_global_device_ids=true | all-gather | bytes 81920 | tf_op jit(solution)/shard_map/all_gather | solution.py:157
  64.3 13.3 %all-gather = f32[32,8,128]{2,1,0:T(8,128)S(1)} all-gather(f32[8,8,128]{2,1,0:T(8,128)S(1)} %pad_maximum_fusion.7), channel_id=2, replica_groups=mesh['span'=8,'wall'=4] {'wall'}, dimensions={0}, use_global_device_ids=true | all-gather | bytes 163840 | tf_op jit(solution)/shard_map/all_gather | solution.py:156
  77.8 0.4 fusion
  78.3 2.5 %copy.39 = f32[4,8,128,128]{3,2,1,0:T(8,128)} copy(f32[4,8,128,128]{3,1,0,2:T(8,128)S(1)} %fusion) | data formatting | bytes 4194304
  (59 shorter events, 3.0 us)
Async XLA Ops:
  4.0 5.2 %copy-start.1 = (f32[8,128,128]{2,1,0:T(8,128)S(1)}, f32[8,128,128]{2,1,0:T(8,128)}, u32[]{:S(2)}) copy-start(f32[8,128,128]{2,1,0:T(8,128)} %param.3) | copy-start | bytes 1572868
  5.8 15.0 %collective-permute-start.1 = (f32[4,2,128,128]{3,1,0,2:T(2,128)}, f32[4,2,128,128]{3,1,0,2:T(2,128)}, u32[]{:S(2)}, u32[]{:S(2)}) collective-permute-start(f32[4,2,128,128]{3,1,0,2:T(2,128)} %get-tuple-element.90), channel_id=1, source_target_pairs={{4,0},{8,4},{12,8},{16,12},{20,16},{24,20},{28,24},{0,28},{5,1},{9... | collective-permute-start | bytes 1572872 | tf_op jit(solution)/shard_map/ppermute | solution.py:25
  9.2 13.7 %collective-permute-start = (f32[4,2,128,128]{3,1,0,2:T(2,128)}, f32[4,2,128,128]{3,1,0,2:T(2,128)}, u32[]{:S(2)}, u32[]{:S(2)}) collective-permute-start(f32[4,2,128,128]{3,1,0,2:T(2,128)} %get-tuple-element.89), channel_id=1, source_target_pairs={{0,4},{4,8},{8,12},{12,16},{16,20},{20,24},{24,28},{28,0},{1,5},{5... | collective-permute-start | bytes 1572872 | tf_op jit(solution)/shard_map/ppermute | solution.py:22
  9.2 4.8 %collective-permute-start.2 = (f32[8,1,128]{2,0,1:T(8,128)S(1)}, f32[8,1,128]{2,0,1:T(8,128)S(1)}, u32[]{:S(2)}, u32[]{:S(2)}) collective-permute-start(f32[8,1,128]{2,0,1:T(8,128)S(1)} %copy.46), channel_id=1, source_target_pairs={{0,1},{1,2},{2,3},{4,5},{5,6},{6,7},{8,9},{9,10},{10,11},{12,13},{... | collective-permute-start | bytes 12296 | tf_op jit(solution)/shard_map/ppermute | solution.py:13
  32.0 2.3 %copy-start = (f32[4,8,128,128]{3,2,1,0:T(8,128)S(1)}, f32[4,8,128,128]{3,2,1,0:T(8,128)}, u32[]{:S(2)}) copy-start(f32[4,8,128,128]{3,2,1,0:T(8,128)} %param.2) | copy-start | bytes 6291460
  48.2 1.0 %copy-start.2 = (f32[8,128,128]{2,0,1:T(8,128)S(1)}, f32[8,128,128]{2,0,1:T(8,128)}, u32[]{:S(2)}) copy-start(f32[8,128,128]{2,0,1:T(8,128)} %get-tuple-element.25) | copy-start | bytes 1572868
  48.2 1.2 %copy-start.3 = (f32[8,128,128]{2,0,1:T(8,128)S(1)}, f32[8,128,128]{2,0,1:T(8,128)}, u32[]{:S(2)}) copy-start(f32[8,128,128]{2,0,1:T(8,128)} %get-tuple-element.26) | copy-start | bytes 1572868
where the time goes:
time: 81 us; the launch traced here: 80.8 us
  other arithmetic  28.2 us (35%)
  blocking collectives  26.9 us (33%)
  local copies, waits for them, and re-layouts  13.8 us (17%)
  starting transfers between devices  6.85 us (8%)
  waiting for transfers between devices  3.96 us (5%)
  between operations  1.18 us (1%)
    all_gather x1, blocking collectives, solve_segments(): lax.all_gather(coupling_local, 'wall', axis=0, tiled=True)  13.5 us
    all_gather x1, blocking collectives, solve_segments(): lax.all_gather(ends_local, 'wall', axis=0, tiled=True)  13.3 us
    unnamed x13, local copies, waits for them, and re-layouts  9.18 us
    sub x6, other arithmetic, reduce_lines(): rhs_stack = rhs_stack - left_factor * rhs_low - right_factor * rhs_high  6.57 us
    add x3, other arithmetic, directed(): node_terms[0][power_index] + node_terms[1][power_index]  3.55 us
    ppermute x1, starting transfers between devices, passed_along(): return lax.ppermute(block, axis, route)  3.48 us
    ppermute x1, starting transfers between devices, padded(): lax.ppermute(lax.slice_in_dim(block, 0, width, axis=dim), axis, backward)  3.36 us
    slice x14, local copies, waits for them, and re-layouts, shifted_rows(): values[..., :row_count - offset, :]  3.29 us
  transfers between devices with their start and end apart: 3, of which 3 were waited for; matrix products, arithmetic and copies ran while one was open for 7% of the time, Pallas kernels for 0%

commit v1 on v0

v1 whole, which is shorter than its diff:
```python
import functools

import jax
import jax.numpy as jnp
from jax import lax
from jax.experimental import pallas as pl
from jax.experimental.pallas import tpu as pltpu
from jax.sharding import PartitionSpec as P

courant = 0.2
diffusion_number = 20000.0
VMEM_LIMIT = 60 * 1024 * 1024


def quadrature(m0, m1, m2, m3):
    inverse = 1.0 / m0
    mean = m1 * inverse
    ratio_two = m2 * inverse
    central_two = ratio_two - mean * mean
    central_three = m3 * inverse - 3.0 * mean * ratio_two + 2.0 * mean * mean * mean
    half_skew = 0.5 * (central_three / central_two)
    square = half_skew * half_skew + central_two
    inverse_root = lax.rsqrt(square)
    root = square * inverse_root
    scale = m0 * (0.5 * inverse_root)
    low = half_skew - root
    high = half_skew + root
    return (scale * high, -scale * low, mean + low, mean + high)


def half_slope(below, centre, above):
    first = above - centre
    second = centre - below
    return 0.5 * (
        jnp.maximum(jnp.minimum(first, second), 0.0) + jnp.minimum(jnp.maximum(first, second), 0.0)
    )


def directed(state, outgoing):
    total = None
    for node in range(2):
        speed = state[node + 2]
        carried = jnp.maximum(speed, 0.0) if outgoing else jnp.minimum(speed, 0.0)
        term = state[node] * carried
        terms = [term]
        for _ in range(3):
            term = term * speed
            terms.append(term)
        total = terms if total is None else [a + b for a, b in zip(total, terms)]
    return total


def transport_kernel(
    n_span, n_wall, chunk,
    m_hbm, k_hbm,
    ts, hs, us, vs, ends,
    ms, lo, hi, ks, coef_g, rhs_g, starts,
    own_sem, halo_send, halo_recv, coef_send, coef_recv, rhs_send, rhs_recv,
):
    planes, rows, width = m_hbm.shape[1], m_hbm.shape[2], m_hbm.shape[3]
    pitch = ts.shape[1] // planes
    chunks = rows // chunk
    me_s = lax.axis_index("span")
    me_w = lax.axis_index("wall")
    right = lax.rem(me_s + 1, n_span)
    left = lax.rem(me_s + n_span - 1, n_span)

    own_k = pltpu.make_async_copy(k_hbm, ks.reshape(planes, pitch, width).at[:, pl.ds(0, rows), :], own_sem.at[0])
    own_k.start()
    own_m = pltpu.make_async_copy(m_hbm, ms, own_sem.at[1])
    own_m.start()

    barrier = pltpu.get_barrier_semaphore()
    for other in (left, right):
        pl.semaphore_signal(barrier, inc=1, device_id={"span": other}, device_id_type=pl.DeviceIdType.MESH)
    for step in range(1, n_wall):
        pl.semaphore_signal(
            barrier, inc=1, device_id={"wall": lax.rem(me_w + step, n_wall)}, device_id_type=pl.DeviceIdType.MESH
        )
    pl.semaphore_wait(barrier, n_wall + 1)

    def halo_copy(side, c):
        at = pl.ds(pl.multiple_of(c * chunk, 8), chunk)
        first = planes - 2 if side == 0 else 0
        return pltpu.make_async_remote_copy(
            src_ref=m_hbm.at[:, pl.ds(first, 2), at, :],
            dst_ref=(lo if side == 0 else hi).at[:, :, at, :],
            send_sem=halo_send.at[side, c],
            recv_sem=halo_recv.at[side, c],
            device_id={"span": right if side == 0 else left},
            device_id_type=pl.DeviceIdType.MESH,
        )

    def wall_copy(buffer, send, recv, step):
        return pltpu.make_async_remote_copy(
            src_ref=buffer.at[me_w],
            dst_ref=buffer.at[me_w],
            send_sem=send.at[step - 1],
            recv_sem=recv.at[step - 1],
            device_id={"wall": lax.rem(me_w + step, n_wall)},
            device_id_type=pl.DeviceIdType.MESH,
        )

    def start_halo(c, _):
        halo_copy(0, c).start()
        halo_copy(1, c).start()
        return 0

    lax.fori_loop(0, chunks, start_halo, 0)

    own_k.wait()
    zero = jnp.zeros((planes, width), jnp.float32)
    one = jnp.ones((planes, width), jnp.float32)

    def line_row(step, carry):
        v, phi, v_sum, u, psi, u_sum = carry
        for i in range(8):
            j = step * 8 + i
            vs[j] = v
            phi = phi + v
            v_sum = v_sum + v
            v = v + phi * (1.0 / (diffusion_number * ks[pl.ds(j, planes, stride=pitch), :]))
            b = rows - 1 - j
            psi = psi + u
            u = u + psi * (1.0 / (diffusion_number * ks[pl.ds(b, planes, stride=pitch), :]))
            us[b] = u
            u_sum = u_sum + u
        return (v, phi, v_sum, u, psi, u_sum)

    v_end, _, v_sum, u_end, _, u_sum = lax.fori_loop(
        0, rows // 8, line_row, (zero, one, zero, zero, one, zero)
    )
    through = 1.0 / v_end
    norm = 1.0 / u_end
    coef_g[me_w, 0] = through
    coef_g[me_w, 1] = u_sum * norm
    coef_g[me_w, 2] = v_sum * through
    for step in range(1, n_wall):
        wall_copy(coef_g, coef_send, coef_recv, step).start()

    def scale_row(step, _):
        for i in range(8):
            us[step * 8 + i] = us[step * 8 + i] * norm
        return 0

    lax.fori_loop(0, rows // 8, scale_row, 0)
    own_m.wait()

    def group(index, carry):
        base = pl.multiple_of(index * 8, 8)
        at = pl.ds(base, 8)

        def cell(p):
            if p < 0:
                return [lo[k, p + 2, at, :] for k in range(4)]
            if p >= planes:
                return [hi[k, p - planes, at, :] for k in range(4)]
            return [ms[k, p, at, :] for k in range(4)]

        below = None
        centre = quadrature(*cell(-2))
        above = quadrature(*cell(-1))
        going = None
        flux_before = None
        for p in range(-1, planes + 1):
            below, centre, above = centre, above, quadrature(*cell(p + 1))
            slope = [half_slope(b, c, a) for b, c, a in zip(below, centre, above)]
            if p >= 0:
                coming = directed([c - s for c, s in zip(centre, slope)], False)
                flux = [a + b for a, b in zip(going, coming)]
                if p >= 1:
                    for k in range(4):
                        ts[k, pl.ds(pl.multiple_of((p - 1) * pitch + base, 8), 8), :] = ms[k, p - 1, at, :] - courant * (
                            flux[k] - flux_before[k]
                        )
                flux_before = flux
            if p < planes:
                going = directed([c + s for c, s in zip(centre, slope)], True)
        sums_v, sums_u = list(carry[:4]), list(carry[4:])
        for i in range(8):
            v = vs[base + i]
            u = us[base + i]
            for k in range(4):
                t = ts[k, pl.ds(base + i, planes, stride=pitch), :]
                sums_v[k] = sums_v[k] + v * t
                sums_u[k] = sums_u[k] + u * t
                hs[k, base + i] = u * sums_v[k] - v * sums_u[k]
        return tuple(sums_v + sums_u)

    def chunk_step(c, carry):
        halo_copy(0, c).wait_recv()
        halo_copy(1, c).wait_recv()
        for g in range(chunk // 8):
            carry = group(c * (chunk // 8) + g, carry)
        return carry

    sums = lax.fori_loop(0, chunks, chunk_step, (zero,) * 8)
    for k in range(4):
        rhs_g[me_w, k] = sums[4 + k]
        rhs_g[me_w, 4 + k] = sums[k] * through
    for step in range(1, n_wall):
        wall_copy(rhs_g, rhs_send, rhs_recv, step).start()
    for step in range(1, n_wall):
        wall_copy(coef_g, coef_send, coef_recv, step).wait()

    links, inverses = [], []
    held = None
    for s in range(n_wall):
        link = coef_g[s, 0]
        ground = coef_g[s, 1]
        if s > 0:
            ground = ground + coef_g[s - 1, 2] + links[-1] * held * inverses[-1]
        held = ground
        links.append(link)
        inverses.append(1.0 / (held + link))

    for step in range(1, n_wall):
        wall_copy(rhs_g, rhs_send, rhs_recv, step).wait()
    for k in range(4):
        sources = []
        for s in range(n_wall):
            source = rhs_g[s, k]
            if s > 0:
                source = source + rhs_g[s - 1, 4 + k] + links[s - 1] * inverses[s - 1] * sources[-1]
            sources.append(source)
        value = zero
        starts[n_wall, k] = zero
        for s in reversed(range(n_wall)):
            value = (sources[s] + links[s] * value) * inverses[s]
            starts[s, k] = value
    for k in range(4):
        ends[k] = starts[me_w, k]
        ends[4 + k] = sums[4 + k] + through * starts[me_w + 1, k]

    def end_halo(c, _):
        halo_copy(0, c).wait_send()
        halo_copy(1, c).wait_send()
        return 0

    lax.fori_loop(0, chunks, end_halo, 0)


def output_kernel(parts, ts, hs, us, vs, ends, t_hbm, x_hbm, xs, t_sem, x_sem):
    planes, rows, width = t_hbm.shape[1], t_hbm.shape[2], t_hbm.shape[3]
    pitch = ts.shape[1] // planes
    size = rows // parts
    moved = pltpu.make_async_copy(
        ts.reshape(4, planes, pitch, width).at[:, :, pl.ds(0, rows), :], t_hbm, t_sem.at[0]
    )
    moved.start()
    copies = []
    for part in range(parts):

        def row_block(step, _):
            for i in range(8):
                j = part * size + step * 8 + i
                v = vs[j]
                u = us[j]
                for k in range(4):
                    xs[k, pl.ds(j, planes, stride=pitch), :] = hs[k, j] + (u * ends[k] + v * ends[4 + k])
            return 0

        lax.fori_loop(0, size // 8, row_block, 0)
        at = pl.ds(part * size, size)
        copy = pltpu.make_async_copy(
            xs.reshape(4, planes, pitch, width).at[:, :, at, :], x_hbm.at[:, :, at, :], x_sem.at[part]
        )
        copy.start()
        copies.append(copy)
    moved.wait()
    for copy in copies:
        copy.wait()


def body(n_span, n_wall, moments, diffusivity):
    _, planes, rows, width = moments.shape
    pitch = rows + 8
    chunk = 16 if rows % 16 == 0 else 8
    f32 = jnp.float32
    dma = pltpu.SemaphoreType.DMA
    any_spec = pl.BlockSpec(memory_space=pl.ANY)
    vmem_spec = pl.BlockSpec(memory_space=pltpu.VMEM)
    middle = [
        (4, planes * pitch, width),
        (4, rows, planes, width),
        (rows, planes, width),
        (rows, planes, width),
        (8, planes, width),
    ]
    held = pl.pallas_call(
        functools.partial(transport_kernel, n_span, n_wall, chunk),
        out_shape=[pltpu.VMEM(shape, f32) for shape in middle],
        in_specs=[pl.BlockSpec(memory_space=pltpu.HBM)] * 2,
        out_specs=[vmem_spec] * 5,
        scratch_shapes=[
            pltpu.VMEM((4, planes, rows, width), f32),
            pltpu.VMEM((4, 2, rows, width), f32),
            pltpu.VMEM((4, 2, rows, width), f32),
            pltpu.VMEM((planes * pitch, width), f32),
            pltpu.VMEM((n_wall, 3, planes, width), f32),
            pltpu.VMEM((n_wall, 8, planes, width), f32),
            pltpu.VMEM((n_wall + 1, 4, planes, width), f32),
            dma((2,)),
            dma((2, rows // chunk)),
            dma((2, rows // chunk)),
            dma((n_wall - 1,)),
            dma((n_wall - 1,)),
            dma((n_wall - 1,)),
            dma((n_wall - 1,)),
        ],
        compiler_params=pltpu.CompilerParams(collective_id=0, has_side_effects=True, vmem_limit_bytes=24 << 20),
        name="transport",
    )(moments, diffusivity)
    parts = 4
    out = jax.ShapeDtypeStruct(moments.shape, f32)
    return pl.pallas_call(
        functools.partial(output_kernel, parts),
        out_shape=[out, out],
        in_specs=[vmem_spec] * 5,
        out_specs=[any_spec, any_spec],
        scratch_shapes=[pltpu.VMEM((4, planes * pitch, width), f32), dma((1,)), dma((parts,))],
        compiler_params=pltpu.CompilerParams(vmem_limit_bytes=24 << 20),
        name="outputs",
    )(*held)


def solution(mesh):
    in_specs = (P(None, "span", "wall", None), P("span", "wall", None))
    out_specs = (P(None, "span", "wall", None), P(None, "span", "wall", None))
    run = functools.partial(body, mesh.shape["span"], mesh.shape["wall"])
    return jax.shard_map(run, mesh=mesh, in_specs=in_specs, out_specs=out_specs, check_vma=False)
```

time: 81 us -> 28.8 us (0.36)
  other arithmetic: 28.2 us -> 0 us
  blocking collectives: 26.9 us -> 0 us
  Pallas kernels: 0 us -> 25.4 us
  local copies, waits for them, and re-layouts: 13.8 us -> 2.63 us
  starting transfers between devices: 6.85 us -> 0 us
  waiting for transfers between devices: 3.96 us -> 0 us
    all_gather x2 -> x0, blocking collectives: 26.9 us -> none  [the longest x1 13.5 us: solve_segments(): lax.all_gather(coupling_local, 'wall', axis=0, tiled=True)]
    pallas_call x0 -> x2, Pallas kernels: none -> 25.4 us  [the longest x1 23.3 us: body(): pl.pallas_call(functools.partial(transport_kernel, n_span, n_wall, chunk)...]
    sub x20 -> x0, other arithmetic: 14.9 us -> none  [the longest x6 6.57 us: reduce_lines(): rhs_stack = rhs_stack - left_factor * rhs_low - right_factor * rhs_high]
    ppermute x3 -> x0, starting transfers between devices: 6.85 us -> none  [the longest x1 3.48 us: passed_along(): return lax.ppermute(block, axis, route)]
    unnamed x13 -> x4, local copies, waits for them, and re-layouts: 9.18 us -> 2.63 us
    add x5 -> x0, other arithmetic: 5.82 us -> none  [the longest x3 3.55 us: directed(): node_terms[0][power_index] + node_terms[1][power_index]]
    slice x28 -> x0, local copies, waits for them, and re-layouts: 4.17 us -> none  [the longest x14 3.29 us: shifted_rows(): values[..., :row_count - offset, :]]
    ppermute x3 -> x0, waiting for transfers between devices: 3.96 us -> none  [the longest x1 1.98 us: padded(): lax.ppermute(lax.slice_in_dim(block, block.shape[dim] - width, None, axis...]
  transfers between devices with their start and end apart: 3 -> 0, of which waited for: 3 -> 0; matrix products, arithmetic and copies ran while one was open for 7% -> 0% of each run, Pallas kernels for 0% -> 0%
where the time goes in v1:
time: 28.8 us; the launch traced here: 28.6 us
  Pallas kernels  25.4 us (88%)
  local copies, waits for them, and re-layouts  2.63 us (9%)
  between operations  0.65 us (2%)
    pallas_call x1, Pallas kernels, body(): pl.pallas_call(functools.partial(transport_kernel, n_span, n_wall, chunk)...  23.3 us
    unnamed x4, local copies, waits for them, and re-layouts  2.63 us
    pallas_call x1, Pallas kernels, body(): pl.pallas_call(functools.partial(output_kernel, parts), out_shape=[out, o...  2.05 us

profile of v1, /device:TPU:0, one launch (start us, length us, event | category | flops | bytes accessed | tf_op | source)
XLA Modules:
  0.0 28.6 jit_solution(7326585756370250657)
XLA Ops:
  0.6 0.0 copy-start
  0.6 1.6 %copy-done = f32[4,8,128,128]{3,2,1,0:T(8,128)S(1)} copy-done((f32[4,8,128,128]{3,2,1,0:T(8,128)S(1)}, f32[4,8,128,128]{3,2,1,0:T(8,128)}, u32[]{:S(2)}) %copy-start) | copy-done | bytes 2097176
  2.2 0.0 copy-start.1
  2.2 1.0 %copy-done.1 = f32[8,128,128]{2,1,0:T(8,128)S(1)} copy-done((f32[8,128,128]{2,1,0:T(8,128)S(1)}, f32[8,128,128]{2,1,0:T(8,128)}, u32[]{:S(2)}) %copy-start.1) | copy-done | bytes 524312
  3.3 23.3 %transport.1 = (f32[4,1088,128]{2,1,0:T(8,128)S(1)}, f32[4,128,8,128]{3,2,1,0:T(8,128)S(1)}, f32[128,8,128]{2,1,0:T(8,128)S(1)}, f32[128,8,128]{2,1,0:T(8,128)S(1)}, f32[8,8,128]{2,1,0:T(8,128)S(1)}) custom-call(f32[4,8,128,128]{3,2,1,0:T(8,128)S(1)} %copy-done, f32[8,128,128]{2,1,0:T(8,128)S(1)} %copy-done.1), custom_call_target="tpu_custom_call" | custom-call | tf_op jit(solution)/shard_map/transport/pallas_call | solution.py:290
  26.6 2.0 %outputs.1 = (f32[4,8,128,128]{3,2,1,0:T(8,128)}, f32[4,8,128,128]{3,2,1,0:T(8,128)}) custom-call(f32[4,1088,128]{2,1,0:T(8,128)S(1)} %get-tuple-element.7.ts, f32[4,128,8,128]{3,2,1,0:T(8,128)S(1)} %get-tuple-element.8.hs, f32[128,8,128]{2,1,0:T(8,128)S(1)} %get-tuple-element.9.us, f32[128,8,128]{2,1,0:T(8,128)S(1)} %get-tuple-element.10.vs, ...), custom_call_target="tpu_custom_call" | custom-call | tf_op jit(solution)/shard_map/outputs/pallas_call | solution.py:316
Async XLA Ops:
  0.6 1.6 %copy-start = (f32[4,8,128,128]{3,2,1,0:T(8,128)S(1)}, f32[4,8,128,128]{3,2,1,0:T(8,128)}, u32[]{:S(2)}) copy-start(f32[4,8,128,128]{3,2,1,0:T(8,128)} %m_hbm.1) | copy-start | bytes 6291460
  2.2 1.0 %copy-start.1 = (f32[8,128,128]{2,1,0:T(8,128)S(1)}, f32[8,128,128]{2,1,0:T(8,128)}, u32[]{:S(2)}) copy-start(f32[8,128,128]{2,1,0:T(8,128)} %k_hbm.1) | copy-start | bytes 1572868

commit v2 on v1

--- a/solution.py
+++ b/solution.py
@@ -310,7 +310,10 @@
         ],
         compiler_params=pltpu.CompilerParams(collective_id=0, has_side_effects=True, vmem_limit_bytes=24 << 20),
         name="transport",
-    )(moments, diffusivity)
+    )(
+        pltpu.with_memory_space_constraint(moments, pltpu.HBM),
+        pltpu.with_memory_space_constraint(diffusivity, pltpu.HBM),
+    )
     parts = 4
     out = jax.ShapeDtypeStruct(moments.shape, f32)
     return pl.pallas_call(

time: 28.8 us -> 26.2 us (0.910)
  local copies, waits for them, and re-layouts: 2.63 us -> 0 us
    unnamed x4 -> x0, local copies, waits for them, and re-layouts: 2.63 us -> none
where the time goes in v2:
time: 26.2 us; the launch traced here: 26.1 us
  Pallas kernels  25.4 us (97%)
  between operations  0.64 us (2%)
    pallas_call x1, Pallas kernels, body(): pl.pallas_call(functools.partial(transport_kernel, n_span, n_wall, chunk)...  23.4 us
    pallas_call x1, Pallas kernels, body(): pl.pallas_call(functools.partial(output_kernel, parts), out_shape=[out, o...  2.05 us

profile of v2, /device:TPU:0, one launch (start us, length us, event | category | flops | bytes accessed | tf_op | source)
XLA Modules:
  0.0 26.1 jit_solution(18015042505027365658)
XLA Ops:
  0.6 23.4 %transport.1 = (f32[4,1088,128]{2,1,0:T(8,128)S(1)}, f32[4,128,8,128]{3,2,1,0:T(8,128)S(1)}, f32[128,8,128]{2,1,0:T(8,128)S(1)}, f32[128,8,128]{2,1,0:T(8,128)S(1)}, f32[8,8,128]{2,1,0:T(8,128)S(1)}) custom-call(f32[4,8,128,128]{3,2,1,0:T(8,128)} %m_hbm.1, f32[8,128,128]{2,1,0:T(8,128)} %k_hbm.1), custom_call_target="tpu_custom_call" | custom-call | tf_op jit(solution)/shard_map/transport/pallas_call | solution.py:290
  24.0 2.0 %outputs.1 = (f32[4,8,128,128]{3,2,1,0:T(8,128)}, f32[4,8,128,128]{3,2,1,0:T(8,128)}) custom-call(f32[4,1088,128]{2,1,0:T(8,128)S(1)} %get-tuple-element.7.ts, f32[4,128,8,128]{3,2,1,0:T(8,128)S(1)} %get-tuple-element.8.hs, f32[128,8,128]{2,1,0:T(8,128)S(1)} %get-tuple-element.9.us, f32[128,8,128]{2,1,0:T(8,128)S(1)} %get-tuple-element.10.vs, ...), custom_call_target="tpu_custom_call" | custom-call | tf_op jit(solution)/shard_map/outputs/pallas_call | solution.py:319

commit v3 on v2

--- a/solution.py
+++ b/solution.py
@@ -54,7 +54,7 @@
     n_span, n_wall, chunk,
     m_hbm, k_hbm,
     ts, hs, us, vs, ends,
-    ms, lo, hi, ks, coef_g, rhs_g, starts,
+    ms, ks, coef_g, rhs_g, starts,
     own_sem, halo_send, halo_recv, coef_send, coef_recv, rhs_send, rhs_recv,
 ):
     planes, rows, width = m_hbm.shape[1], m_hbm.shape[2], m_hbm.shape[3]
@@ -64,10 +64,11 @@
     me_w = lax.axis_index("wall")
     right = lax.rem(me_s + 1, n_span)
     left = lax.rem(me_s + n_span - 1, n_span)
+    late = lax.rem(me_s, 2)
 
     own_k = pltpu.make_async_copy(k_hbm, ks.reshape(planes, pitch, width).at[:, pl.ds(0, rows), :], own_sem.at[0])
     own_k.start()
-    own_m = pltpu.make_async_copy(m_hbm, ms, own_sem.at[1])
+    own_m = pltpu.make_async_copy(m_hbm, ms.at[:, pl.ds(2, planes)], own_sem.at[1])
     own_m.start()
 
     barrier = pltpu.get_barrier_semaphore()
@@ -81,29 +82,36 @@
 
     def halo_copy(side, c):
         at = pl.ds(pl.multiple_of(c * chunk, 8), chunk)
-        first = planes - 2 if side == 0 else 0
         return pltpu.make_async_remote_copy(
-            src_ref=m_hbm.at[:, pl.ds(first, 2), at, :],
-            dst_ref=(lo if side == 0 else hi).at[:, :, at, :],
+            src_ref=m_hbm.at[:, pl.ds((1 - side) * (planes - 2), 2), at, :],
+            dst_ref=ms.at[:, pl.ds(side * (planes + 2), 2), at, :],
             send_sem=halo_send.at[side, c],
             recv_sem=halo_recv.at[side, c],
-            device_id={"span": right if side == 0 else left},
+            device_id={"span": lax.rem(me_s + 1 + side * (n_span - 2), n_span)},
             device_id_type=pl.DeviceIdType.MESH,
         )
 
-    def wall_copy(buffer, send, recv, step):
+    def wall_copy(buffer, send, recv, step, *at):
+        part = buffer.at[(me_w, *at)]
         return pltpu.make_async_remote_copy(
-            src_ref=buffer.at[me_w],
-            dst_ref=buffer.at[me_w],
+            src_ref=part,
+            dst_ref=part,
             send_sem=send.at[step - 1],
             recv_sem=recv.at[step - 1],
             device_id={"wall": lax.rem(me_w + step, n_wall)},
             device_id_type=pl.DeviceIdType.MESH,
         )
 
+    def sums_copy(stage, step):
+        if stage == 0:
+            at = pl.ds(pl.multiple_of((1 - late) * 16, 8), 8 * (planes - 2))
+        else:
+            at = pl.ds(pl.multiple_of(late * 8 * (planes - 2), 8), 16)
+        return wall_copy(rhs_g, rhs_send.at[stage], rhs_recv.at[stage], step, at)
+
     def start_halo(c, _):
-        halo_copy(0, c).start()
-        halo_copy(1, c).start()
+        halo_copy(1 - late, c).start()
+        halo_copy(late, c).start()
         return 0
 
     lax.fori_loop(0, chunks, start_halo, 0)
@@ -146,36 +154,32 @@
     lax.fori_loop(0, rows // 8, scale_row, 0)
     own_m.wait()
 
-    def group(index, carry):
-        base = pl.multiple_of(index * 8, 8)
+    def transport(base, first, count):
         at = pl.ds(base, 8)
 
         def cell(p):
-            if p < 0:
-                return [lo[k, p + 2, at, :] for k in range(4)]
-            if p >= planes:
-                return [hi[k, p - planes, at, :] for k in range(4)]
-            return [ms[k, p, at, :] for k in range(4)]
+            return [ms[k, first + p + 2, at, :] for k in range(4)]
 
         below = None
         centre = quadrature(*cell(-2))
         above = quadrature(*cell(-1))
         going = None
         flux_before = None
-        for p in range(-1, planes + 1):
+        for p in range(-1, count + 1):
             below, centre, above = centre, above, quadrature(*cell(p + 1))
             slope = [half_slope(b, c, a) for b, c, a in zip(below, centre, above)]
             if p >= 0:
                 coming = directed([c - s for c, s in zip(centre, slope)], False)
                 flux = [a + b for a, b in zip(going, coming)]
                 if p >= 1:
+                    row = pl.ds(pl.multiple_of((first + p - 1) * pitch + base, 8), 8)
                     for k in range(4):
-                        ts[k, pl.ds(pl.multiple_of((p - 1) * pitch + base, 8), 8), :] = ms[k, p - 1, at, :] - courant * (
-                            flux[k] - flux_before[k]
-                        )
+                        ts[k, row, :] = ms[k, first + p + 1, at, :] - courant * (flux[k] - flux_before[k])
                 flux_before = flux
-            if p < planes:
+            if p < count:
                 going = directed([c + s for c, s in zip(centre, slope)], True)
+
+    def add_rows(base, carry, keep):
         sums_v, sums_u = list(carry[:4]), list(carry[4:])
         for i in range(8):
             v = vs[base + i]
@@ -184,22 +188,38 @@
                 t = ts[k, pl.ds(base + i, planes, stride=pitch), :]
                 sums_v[k] = sums_v[k] + v * t
                 sums_u[k] = sums_u[k] + u * t
-                hs[k, base + i] = u * sums_v[k] - v * sums_u[k]
+                if keep:
+                    hs[k, base + i] = u * sums_v[k] - v * sums_u[k]
         return tuple(sums_v + sums_u)
 
-    def chunk_step(c, carry):
-        halo_copy(0, c).wait_recv()
-        halo_copy(1, c).wait_recv()
-        for g in range(chunk // 8):
-            carry = group(c * (chunk // 8) + g, carry)
-        return carry
-
-    sums = lax.fori_loop(0, chunks, chunk_step, (zero,) * 8)
-    for k in range(4):
-        rhs_g[me_w, k] = sums[4 + k]
-        rhs_g[me_w, 4 + k] = sums[k] * through
-    for step in range(1, n_wall):
-        wall_copy(rhs_g, rhs_send, rhs_recv, step).start()
+    def pass_over(stage):
+        first = (1 - late) * 2 if stage == 0 else late * (planes - 2)
+        count = planes - 2 if stage == 0 else 2
+
+        def step(c, carry):
+            halo_copy(1 - late if stage == 0 else late, c).wait_recv()
+            for g in range(chunk // 8):
+                base = pl.multiple_of(c * chunk + g * 8, 8)
+                transport(base, first, count)
+                carry = add_rows(base, carry, stage == 1)
+            return carry
+
+        return lax.fori_loop(0, chunks, step, (zero,) * 8)
+
+    def put_sums(sums):
+        for k in range(4):
+            rhs_g[me_w, pl.ds(k, planes, stride=8), :] = sums[4 + k]
+            rhs_g[me_w, pl.ds(4 + k, planes, stride=8), :] = sums[k] * through
+
+    put_sums(pass_over(0))
+    for step in range(1, n_wall):
+        sums_copy(0, step).start()
+    sums = pass_over(1)
+    for step in range(1, n_wall):
+        sums_copy(0, step).wait()
+    put_sums(sums)
+    for step in range(1, n_wall):
+        sums_copy(1, step).start()
     for step in range(1, n_wall):
         wall_copy(coef_g, coef_send, coef_recv, step).wait()
 
@@ -215,13 +235,17 @@
         inverses.append(1.0 / (held + link))
 
     for step in range(1, n_wall):
-        wall_copy(rhs_g, rhs_send, rhs_recv, step).wait()
+        sums_copy(1, step).wait()
     for k in range(4):
         sources = []
         for s in range(n_wall):
-            source = rhs_g[s, k]
+            source = rhs_g[s, pl.ds(k, planes, stride=8), :]
             if s > 0:
-                source = source + rhs_g[s - 1, 4 + k] + links[s - 1] * inverses[s - 1] * sources[-1]
+                source = (
+                    source
+                    + rhs_g[s - 1, pl.ds(4 + k, planes, stride=8), :]
+                    + links[s - 1] * inverses[s - 1] * sources[-1]
+                )
             sources.append(source)
         value = zero
         starts[n_wall, k] = zero
@@ -293,20 +317,18 @@
         in_specs=[pl.BlockSpec(memory_space=pltpu.HBM)] * 2,
         out_specs=[vmem_spec] * 5,
         scratch_shapes=[
-            pltpu.VMEM((4, planes, rows, width), f32),
-            pltpu.VMEM((4, 2, rows, width), f32),
-            pltpu.VMEM((4, 2, rows, width), f32),
+            pltpu.VMEM((4, planes + 4, rows, width), f32),
             pltpu.VMEM((planes * pitch, width), f32),
             pltpu.VMEM((n_wall, 3, planes, width), f32),
-            pltpu.VMEM((n_wall, 8, planes, width), f32),
+            pltpu.VMEM((n_wall, planes * 8, width), f32),
             pltpu.VMEM((n_wall + 1, 4, planes, width), f32),
             dma((2,)),
             dma((2, rows // chunk)),
             dma((2, rows // chunk)),
             dma((n_wall - 1,)),
             dma((n_wall - 1,)),
-            dma((n_wall - 1,)),
-            dma((n_wall - 1,)),
+            dma((2, n_wall - 1)),
+            dma((2, n_wall - 1)),
         ],
         compiler_params=pltpu.CompilerParams(collective_id=0, has_side_effects=True, vmem_limit_bytes=24 << 20),
         name="transport",

time: 26.2 us -> 25.1 us (0.958)
  Pallas kernels: 25.4 us -> 24.3 us
    pallas_call x1, Pallas kernels: 23.4 us -> 22.3 us  [body(): pl.pallas_call(functools.partial(transport_kernel, n_span, n_wall, chunk)...]
where the time goes in v3:
time: 25.1 us; the launch traced here: 25 us
  Pallas kernels  24.3 us (97%)
  between operations  0.64 us (3%)
    pallas_call x1, Pallas kernels, body(): pl.pallas_call(functools.partial(transport_kernel, n_span, n_wall, chunk)...  22.3 us
    pallas_call x1, Pallas kernels, body(): pl.pallas_call(functools.partial(output_kernel, parts), out_shape=[out, o...  2.05 us

profile of v3, /device:TPU:0, one launch (start us, length us, event | category | flops | bytes accessed | tf_op | source)
XLA Modules:
  0.0 25.0 jit_solution(9374701611952581993)
XLA Ops:
  0.6 22.3 %transport.1 = (f32[4,1088,128]{2,1,0:T(8,128)S(1)}, f32[4,128,8,128]{3,2,1,0:T(8,128)S(1)}, f32[128,8,128]{2,1,0:T(8,128)S(1)}, f32[128,8,128]{2,1,0:T(8,128)S(1)}, f32[8,8,128]{2,1,0:T(8,128)S(1)}) custom-call(f32[4,8,128,128]{3,2,1,0:T(8,128)} %m_hbm.1, f32[8,128,128]{2,1,0:T(8,128)} %k_hbm.1), custom_call_target="tpu_custom_call" | custom-call | tf_op jit(solution)/shard_map/transport/pallas_call | solution.py:314
  22.9 2.0 %outputs.1 = (f32[4,8,128,128]{3,2,1,0:T(8,128)}, f32[4,8,128,128]{3,2,1,0:T(8,128)}) custom-call(f32[4,1088,128]{2,1,0:T(8,128)S(1)} %get-tuple-element.7.ts, f32[4,128,8,128]{3,2,1,0:T(8,128)S(1)} %get-tuple-element.8.hs, f32[128,8,128]{2,1,0:T(8,128)S(1)} %get-tuple-element.9.us, f32[128,8,128]{2,1,0:T(8,128)S(1)} %get-tuple-element.10.vs, ...), custom_call_target="tpu_custom_call" | custom-call | tf_op jit(solution)/shard_map/outputs/pallas_call | solution.py:341

commit v4 on v3

--- a/solution.py
+++ b/solution.py
@@ -109,12 +109,20 @@
             at = pl.ds(pl.multiple_of(late * 8 * (planes - 2), 8), 16)
         return wall_copy(rhs_g, rhs_send.at[stage], rhs_recv.at[stage], step, at)
 
-    def start_halo(c, _):
-        halo_copy(1 - late, c).start()
-        halo_copy(late, c).start()
-        return 0
-
-    lax.fori_loop(0, chunks, start_halo, 0)
+    direct = lax.rem(lax.div(me_s, 2) + me_s, 2)
+
+    def start_halo(side):
+        def start(c, _):
+            halo_copy(side, c).start()
+            return 0
+
+        lax.fori_loop(0, chunks, start, 0)
+
+    @pl.when(direct == 0)
+    def _():
+        start_halo(1 - late)
+
+    start_halo(late)
 
     own_k.wait()
     zero = jnp.zeros((planes, width), jnp.float32)
@@ -153,6 +161,10 @@
 
     lax.fori_loop(0, rows // 8, scale_row, 0)
     own_m.wait()
+
+    @pl.when(direct == 1)
+    def _():
+        start_halo(1 - late)
 
     def transport(base, first, count):
         at = pl.ds(base, 8)

time: 25.1 us -> 24.2 us (0.964)
  the two profiles are of different devices: /device:TPU:0 before, /device:TPU:1 now
where the time goes in v4:
time: 24.2 us; the launch traced here: 24.1 us
  Pallas kernels  23.4 us (97%)
  between operations  0.64 us (3%)
    pallas_call x1, Pallas kernels, body(): pl.pallas_call(functools.partial(transport_kernel, n_span, n_wall, chunk)...  21.4 us
    pallas_call x1, Pallas kernels, body(): pl.pallas_call(functools.partial(output_kernel, parts), out_shape=[out, o...  2.05 us

profile of v4, /device:TPU:1, one launch (start us, length us, event | category | flops | bytes accessed | tf_op | source)
XLA Modules:
  0.0 24.1 jit_solution(14576165423285625271)
XLA Ops:
  0.6 21.4 %transport.1 = (f32[4,1088,128]{2,1,0:T(8,128)S(1)}, f32[4,128,8,128]{3,2,1,0:T(8,128)S(1)}, f32[128,8,128]{2,1,0:T(8,128)S(1)}, f32[128,8,128]{2,1,0:T(8,128)S(1)}, f32[8,8,128]{2,1,0:T(8,128)S(1)}) custom-call(f32[4,8,128,128]{3,2,1,0:T(8,128)} %m_hbm.1, f32[8,128,128]{2,1,0:T(8,128)} %k_hbm.1), custom_call_target="tpu_custom_call" | custom-call | tf_op jit(solution)/shard_map/transport/pallas_call | solution.py:326
  22.0 2.0 %outputs.1 = (f32[4,8,128,128]{3,2,1,0:T(8,128)}, f32[4,8,128,128]{3,2,1,0:T(8,128)}) custom-call(f32[4,1088,128]{2,1,0:T(8,128)S(1)} %get-tuple-element.7.ts, f32[4,128,8,128]{3,2,1,0:T(8,128)S(1)} %get-tuple-element.8.hs, f32[128,8,128]{2,1,0:T(8,128)S(1)} %get-tuple-element.9.us, f32[128,8,128]{2,1,0:T(8,128)S(1)} %get-tuple-element.10.vs, ...), custom_call_target="tpu_custom_call" | custom-call | tf_op jit(solution)/shard_map/outputs/pallas_call | solution.py:353

commit v5 on v4

--- a/solution.py
+++ b/solution.py
@@ -53,8 +53,8 @@
 def transport_kernel(
     n_span, n_wall, chunk,
     m_hbm, k_hbm,
-    ts, hs, us, vs, ends,
-    ms, ks, coef_g, rhs_g, starts,
+    ts, xs, un, vn, ends,
+    ms, ks, hs, us, vs, coef_g, rhs_g, last_g, starts,
     own_sem, halo_send, halo_recv, coef_send, coef_recv, rhs_send, rhs_recv,
 ):
     planes, rows, width = m_hbm.shape[1], m_hbm.shape[2], m_hbm.shape[3]
@@ -103,11 +103,7 @@
         )
 
     def sums_copy(stage, step):
-        if stage == 0:
-            at = pl.ds(pl.multiple_of((1 - late) * 16, 8), 8 * (planes - 2))
-        else:
-            at = pl.ds(pl.multiple_of(late * 8 * (planes - 2), 8), 16)
-        return wall_copy(rhs_g, rhs_send.at[stage], rhs_recv.at[stage], step, at)
+        return wall_copy(rhs_g if stage == 0 else last_g, rhs_send.at[stage], rhs_recv.at[stage], step)
 
     direct = lax.rem(lax.div(me_s, 2) + me_s, 2)
 
@@ -230,6 +226,8 @@
     for step in range(1, n_wall):
         sums_copy(0, step).wait()
     put_sums(sums)
+    late_rows = pl.ds(pl.multiple_of(late * 8 * (planes - 2), 8), 16)
+    last_g[me_w] = rhs_g[me_w, late_rows, :]
     for step in range(1, n_wall):
         sums_copy(1, step).start()
     for step in range(1, n_wall):
@@ -246,27 +244,51 @@
         links.append(link)
         inverses.append(1.0 / (held + link))
 
+    def solve_ends():
+        for k in range(4):
+            sources = []
+            for s in range(n_wall):
+                source = rhs_g[s, pl.ds(k, planes, stride=8), :]
+                if s > 0:
+                    source = (
+                        source
+                        + rhs_g[s - 1, pl.ds(4 + k, planes, stride=8), :]
+                        + links[s - 1] * inverses[s - 1] * sources[-1]
+                    )
+                sources.append(source)
+            value = zero
+            starts[n_wall, k] = zero
+            for s in reversed(range(n_wall)):
+                value = (sources[s] + links[s] * value) * inverses[s]
+                starts[s, k] = value
+        for k in range(4):
+            ends[k] = starts[me_w, k]
+            ends[4 + k] = sums[4 + k] + through * starts[me_w + 1, k]
+
+    solve_ends()
+    plane = lax.broadcasted_iota(jnp.int32, (planes, width), 0)
+    first_late = late * (planes - 2)
+    early = jnp.logical_or(plane < first_late, plane >= first_late + 2)
+    known = [jnp.where(early, ends[k], 0.0) for k in range(8)]
+
+    def early_rows(step, _):
+        for i in range(8):
+            j = step * 8 + i
+            at = pl.ds(j, planes, stride=pitch)
+            v = vs[j]
+            u = us[j]
+            un[at, :] = u
+            vn[at, :] = v
+            for k in range(4):
+                xs[k, at, :] = hs[k, j] + (u * known[k] + v * known[4 + k])
+        return 0
+
+    lax.fori_loop(0, rows // 8, early_rows, 0)
     for step in range(1, n_wall):
         sums_copy(1, step).wait()
-    for k in range(4):
-        sources = []
-        for s in range(n_wall):
-            source = rhs_g[s, pl.ds(k, planes, stride=8), :]
-            if s > 0:
-                source = (
-                    source
-                    + rhs_g[s - 1, pl.ds(4 + k, planes, stride=8), :]
-                    + links[s - 1] * inverses[s - 1] * sources[-1]
-                )
-            sources.append(source)
-        value = zero
-        starts[n_wall, k] = zero
-        for s in reversed(range(n_wall)):
-            value = (sources[s] + links[s] * value) * inverses[s]
-            starts[s, k] = value
-    for k in range(4):
-        ends[k] = starts[me_w, k]
-        ends[4 + k] = sums[4 + k] + through * starts[me_w + 1, k]
+    for s in range(n_wall):
+        rhs_g[s, late_rows, :] = last_g[s]
+    solve_ends()
 
     def end_halo(c, _):
         halo_copy(0, c).wait_send()
@@ -276,36 +298,31 @@
     lax.fori_loop(0, chunks, end_halo, 0)
 
 
-def output_kernel(parts, ts, hs, us, vs, ends, t_hbm, x_hbm, xs, t_sem, x_sem):
+def output_kernel(ts, xs, un, vn, ends, t_hbm, x_hbm, last, t_sem, x_sem):
     planes, rows, width = t_hbm.shape[1], t_hbm.shape[2], t_hbm.shape[3]
     pitch = ts.shape[1] // planes
-    size = rows // parts
-    moved = pltpu.make_async_copy(
-        ts.reshape(4, planes, pitch, width).at[:, :, pl.ds(0, rows), :], t_hbm, t_sem.at[0]
-    )
-    moved.start()
-    copies = []
-    for part in range(parts):
-
-        def row_block(step, _):
-            for i in range(8):
-                j = part * size + step * 8 + i
-                v = vs[j]
-                u = us[j]
-                for k in range(4):
-                    xs[k, pl.ds(j, planes, stride=pitch), :] = hs[k, j] + (u * ends[k] + v * ends[4 + k])
-            return 0
-
-        lax.fori_loop(0, size // 8, row_block, 0)
-        at = pl.ds(part * size, size)
-        copy = pltpu.make_async_copy(
-            xs.reshape(4, planes, pitch, width).at[:, :, at, :], x_hbm.at[:, :, at, :], x_sem.at[part]
-        )
+    late = lax.rem(lax.axis_index("span"), 2)
+    early = pl.ds((1 - late) * 2, planes - 2)
+    first = late * (planes - 2)
+    whole = (4, planes, pitch, width)
+    copies = [
+        pltpu.make_async_copy(xs.reshape(whole).at[:, early, pl.ds(0, rows), :], x_hbm.at[:, early], x_sem.at[0]),
+        pltpu.make_async_copy(ts.reshape(whole).at[:, :, pl.ds(0, rows), :], t_hbm, t_sem.at[0]),
+    ]
+    for copy in copies:
         copy.start()
-        copies.append(copy)
-    moved.wait()
-    for copy in copies:
-        copy.wait()
+    for p in range(2):
+        lows = [jnp.broadcast_to(ends[k, pl.ds(first + p, 1), :], (8, width)) for k in range(8)]
+        for block in range(rows // 8):
+            at = pl.ds(pl.multiple_of((first + p) * pitch + block * 8, 8), 8)
+            u = un[at, :]
+            v = vn[at, :]
+            for k in range(4):
+                last[k, p, pl.ds(block * 8, 8), :] = xs[k, at, :] + (u * lows[k] + v * lows[4 + k])
+    copy = pltpu.make_async_copy(last, x_hbm.at[:, pl.ds(first, 2)], x_sem.at[1])
+    copy.start()
+    for other in copies + [copy]:
+        other.wait()
 
 
 def body(n_span, n_wall, moments, diffusivity):
@@ -318,9 +335,9 @@
     vmem_spec = pl.BlockSpec(memory_space=pltpu.VMEM)
     middle = [
         (4, planes * pitch, width),
-        (4, rows, planes, width),
-        (rows, planes, width),
-        (rows, planes, width),
+        (4, planes * pitch, width),
+        (planes * pitch, width),
+        (planes * pitch, width),
         (8, planes, width),
     ]
     held = pl.pallas_call(
@@ -331,8 +348,12 @@
         scratch_shapes=[
             pltpu.VMEM((4, planes + 4, rows, width), f32),
             pltpu.VMEM((planes * pitch, width), f32),
+            pltpu.VMEM((4, rows, planes, width), f32),
+            pltpu.VMEM((rows, planes, width), f32),
+            pltpu.VMEM((rows, planes, width), f32),
             pltpu.VMEM((n_wall, 3, planes, width), f32),
             pltpu.VMEM((n_wall, planes * 8, width), f32),
+            pltpu.VMEM((n_wall, 16, width), f32),
             pltpu.VMEM((n_wall + 1, 4, planes, width), f32),
             dma((2,)),
             dma((2, rows // chunk)),
@@ -348,14 +369,13 @@
         pltpu.with_memory_space_constraint(moments, pltpu.HBM),
         pltpu.with_memory_space_constraint(diffusivity, pltpu.HBM),
     )
-    parts = 4
     out = jax.ShapeDtypeStruct(moments.shape, f32)
     return pl.pallas_call(
-        functools.partial(output_kernel, parts),
+        output_kernel,
         out_shape=[out, out],
         in_specs=[vmem_spec] * 5,
         out_specs=[any_spec, any_spec],
-        scratch_shapes=[pltpu.VMEM((4, planes * pitch, width), f32), dma((1,)), dma((parts,))],
+        scratch_shapes=[pltpu.VMEM((4, 2, rows, width), f32), dma((1,)), dma((2,))],
         compiler_params=pltpu.CompilerParams(vmem_limit_bytes=24 << 20),
         name="outputs",
     )(*held)

time: 24.2 us -> 24.2 us (level)
  no operation moved by 1% of the time
where the time goes in v5:
time: 24.2 us; the launch traced here: 24.1 us
  Pallas kernels  23.4 us (97%)
  between operations  0.64 us (3%)
    pallas_call x1, Pallas kernels, body(): pl.pallas_call(functools.partial(transport_kernel, n_span, n_wall, chunk)...  21.4 us
    pallas_call x1, Pallas kernels, body(): pl.pallas_call(output_kernel, out_shape=[out, out], in_specs=[vmem_spec]...  2.04 us

profile of v5, /device:TPU:1, one launch (start us, length us, event | category | flops | bytes accessed | tf_op | source)
XLA Modules:
  0.0 24.1 jit_solution(14545597444189121231)
XLA Ops:
  0.6 21.4 %transport.1 = (f32[4,1088,128]{2,1,0:T(8,128)S(1)}, f32[4,1088,128]{2,1,0:T(8,128)S(1)}, f32[1088,128]{1,0:T(8,128)S(1)}, f32[1088,128]{1,0:T(8,128)S(1)}, f32[8,8,128]{2,1,0:T(8,128)S(1)}) custom-call(f32[4,8,128,128]{3,2,1,0:T(8,128)} %m_hbm.1, f32[8,128,128]{2,1,0:T(8,128)} %k_hbm.1), custom_call_target="tpu_custom_call" | custom-call | tf_op jit(solution)/shard_map/transport/pallas_call | solution.py:343
  22.0 2.0 %outputs.1 = (f32[4,8,128,128]{3,2,1,0:T(8,128)}, f32[4,8,128,128]{3,2,1,0:T(8,128)}) custom-call(f32[4,1088,128]{2,1,0:T(8,128)S(1)} %get-tuple-element.7.ts, f32[4,1088,128]{2,1,0:T(8,128)S(1)} %get-tuple-element.8.xs, f32[1088,128]{1,0:T(8,128)S(1)} %get-tuple-element.9.un, f32[1088,128]{1,0:T(8,128)S(1)} %get-tuple-element.10.vn, ...), custom_call_target="tpu_custom_call" | custom-call | tf_op jit(solution)/shard_map/outputs/pallas_call | solution.py:373
